TPU v7x, 256 devices: a whole 4x4x8 slice. The times are simulated.
256 devices in a mesh: seq: 32 (over x, z_lo, core), dp: 8 (over z_hi, y).
Axes of the slice: x: 4, y: 4, z: 8 (z_hi: 2, z_lo: 4; z = z_hi * 4 + z_lo), core: 2. Of those that a mesh axis runs over, the one named last changes fastest.
Arguments:
- tokens: bfloat16 [8, 16384, 1536], P('dp', 'seq'), may hold values from -6 to 6
- cotangent: bfloat16 [8, 16384, 1536], P('dp', 'seq'), may hold values from -6 to 6
- conv_weight: float32 [3, 1536], replicated, may hold values from -3.5 to 3.5
- gate_weight: bfloat16 [1536, 1536], P('seq'), may hold values from -0.15625 to 0.15625
- leading_block_factor: bfloat16 [128, 128, 128], P('seq'), may hold values from -0.5 to 0.5
- trailing_block_factor: bfloat16 [128, 128, 128], P('seq'), may hold values from -0.5 to 0.5
Outputs:
- mixed: bfloat16 [8, 16384, 1536], P('dp', 'seq')
- grad_tokens: bfloat16 [8, 16384, 1536], P('dp', 'seq')
- grad_conv: float32 [3, 1536], replicated
- grad_gate: float32 [1536, 1536], P('seq')
- grad_first: float32 [128, 128, 128], P('seq')
- trailing_factor_gradient: float32 [128, 128, 128], P('seq')
All inputs are finite; a program needn't handle non-finite values.
Results may differ from a plain program's by a relative error of at most 0.0067.
Values may be sent and summed in bfloat16 or wider, within the bound.
No kernel may reach another device: no remote copies, remote signals or barrier semaphores. Data moves between devices by JAX's collectives and lax.ppermute only.
A program may use at most 128 MiB of HBM per device.

v0:
```python
import jax
import jax.numpy as jnp
from jax import lax
from jax.sharding import PartitionSpec as P


def with_halo(array, sides, width):
    for axis, dim in sides:
        count, length = (lax.axis_size(axis), array.shape[dim])
        up = [(i, (i + 1) % count) for i in range(count - 1)]
        down = [(j, i) for i, j in up]
        last = lax.slice_in_dim(array, length - width, length, axis=dim)
        first = lax.slice_in_dim(array, 0, width, axis=dim)
        before = lax.ppermute(last, axis, up)
        after = lax.ppermute(first, axis, down)
        array = jnp.concatenate([before, array, after], axis=dim)
    return array


def extend(values):
    return with_halo(values, (("seq", 0),), 1)


def regroup(values):
    return lax.all_to_all(values, "seq", split_axis=0, concat_axis=1, tiled=True)


def shards(
    tokens, cotangent, conv_weight, gate_weight, leading_block_factor, trailing_block_factor
):
    features = tokens[0]
    grad_out = cotangent[0]
    tok_rows = features.shape[0]
    feat_width = features.shape[1]
    local_blocks = leading_block_factor.shape[0]
    block_size = leading_block_factor.shape[1]
    feat_wide = features.astype(jnp.float32)
    pad_feat = extend(features).astype(jnp.float32)
    conv_in = (
        conv_weight[0] * pad_feat[:-2] + conv_weight[1] * feat_wide + conv_weight[2] * pad_feat[2:]
    ).astype(jnp.bfloat16)
    convolution_block_list = conv_in.reshape(local_blocks, block_size, feat_width)
    leading_output = jnp.einsum(
        "shz,szy->hsy",
        leading_block_factor,
        convolution_block_list,
        preferred_element_type=jnp.float32,
    ).astype(jnp.bfloat16)
    column_layout = regroup(leading_output)
    trailing_output = jnp.einsum(
        "vpn,vnu->pvu", trailing_block_factor, column_layout, preferred_element_type=jnp.float32
    ).astype(jnp.bfloat16)
    monarch = regroup(trailing_output).reshape(tok_rows, feat_width)
    whole_gate = lax.all_gather(gate_weight, "seq", axis=0, tiled=True)
    gate_act = jnp.dot(features, whole_gate, preferred_element_type=jnp.float32)
    mon_wide = monarch.astype(jnp.float32)
    grad_wide = grad_out.astype(jnp.float32)
    mixed = (mon_wide * gate_act).astype(jnp.bfloat16)
    d_monarch = (grad_wide * gate_act).astype(jnp.bfloat16)
    d_gate = (grad_wide * mon_wide).astype(jnp.bfloat16)
    second_factor_delta = lax.all_to_all(
        d_monarch.reshape(local_blocks, block_size, feat_width),
        "seq",
        split_axis=1,
        concat_axis=0,
        tiled=True,
    )
    d_inner = jnp.einsum(
        "ica,cid->aid",
        trailing_block_factor,
        second_factor_delta,
        preferred_element_type=jnp.float32,
    ).astype(jnp.bfloat16)
    trailing_factor_gradient = jnp.einsum(
        "wxn,xon->xwo", second_factor_delta, column_layout, preferred_element_type=jnp.float32
    )
    d_first = regroup(d_inner)
    d_conv = (
        jnp.einsum(
            "aib,aid->abd", leading_block_factor, d_first, preferred_element_type=jnp.float32
        )
        .astype(jnp.bfloat16)
        .reshape(tok_rows, feat_width)
    )
    grad_first = jnp.einsum(
        "aid,abd->aib", d_first, convolution_block_list, preferred_element_type=jnp.float32
    )
    d_convw = d_conv.astype(jnp.float32)
    conv_part = jnp.stack(
        [
            jnp.sum(d_convw * pad_feat[:-2], axis=0),
            jnp.sum(d_convw * feat_wide, axis=0),
            jnp.sum(d_convw * pad_feat[2:], axis=0),
        ]
    )
    pad_grad = extend(d_conv).astype(jnp.float32)
    conv_back = (
        conv_weight[0] * pad_grad[2:] + conv_weight[1] * d_convw + conv_weight[2] * pad_grad[:-2]
    )
    gate_back = lax.dot_general(
        d_gate, whole_gate, (((1,), (1,)), ((), ())), preferred_element_type=jnp.float32
    )
    grad_tokens = (conv_back + gate_back).astype(jnp.bfloat16)
    weight_part = lax.psum_scatter(
        lax.dot_general(
            features, d_gate, (((0,), (0,)), ((), ())), preferred_element_type=jnp.float32
        ),
        "seq",
        scatter_dimension=0,
        tiled=True,
    )
    grad_first, trailing_factor_gradient = lax.psum((grad_first, trailing_factor_gradient), "dp")
    grad_gate = lax.psum(weight_part, "dp")
    grad_conv = lax.psum(conv_part, ("seq", "dp"))
    return (
        mixed[None],
        grad_tokens[None],
        grad_conv,
        grad_gate,
        grad_first,
        trailing_factor_gradient,
    )


def solution(mesh):
    return jax.shard_map(
        shards,
        mesh=mesh,
        in_specs=(
            P("dp", "seq", None),
            P("dp", "seq", None),
            P(),
            P("seq", None),
            P("seq", None, None),
            P("seq", None, None),
        ),
        out_specs=(
            P("dp", "seq", None),
            P("dp", "seq", None),
            P(),
            P("seq", None),
            P("seq", None, None),
            P("seq", None, None),
        ),
        check_vma=False,
    )
```

profile of v0, /device:TPU:2, one launch (start us, length us, event | category | flops | bytes accessed | tf_op | source)
XLA Modules:
  0.0 599.1 jit_solution(1992488106284117112)
XLA Ops:
  7.2 0.7 all-gather.2.cloned.1.call-update
  7.9 68.7 %all-gather.2.cloned.1.call-done = bf16[1536,1536]{1,0:T(8,128)(2,1)} async-done(((bf16[48,1536]{1,0:T(8,128)(2,1)}), bf16[1536,1536]{1,0:T(8,128)(2,1)}) %all-gather.2.cloned.1.call-update) | async-done | bytes 4718608 | tf_op jit(solution)/shard_map/all_gather | solution.py:54
  76.6 7.6 %fusion.2 = (bf16[512,1536]{1,0:T(8,128)(2,1)S(1)}, f32[512,1536]{1,0:T(8,128)}) fusion(bf16[1,512,1536]{2,1,0:T(8,128)(2,1)} %param.7, bf16[1536,1536]{1,0:T(8,128)(2,1)} %all-gather.2.cloned.1.call-done, bf16[1,512,1536]{2,1,0:T(8,128)(2,1)} %param.6), kind=kOutput, calls=%fused_computation.9 | convolution fusion | flops 2418278400 | bytes 12582912 | tf_op jit(solution)/shard_map/dot_general | solution.py:55
  84.2 1.2 copy.58
  85.4 42.4 %all_to_all.63 = bf16[4,128,1536]{2,0,1:T(4,128)(2,1)S(1)} all-to-all(bf16[4,128,1536]{2,0,1:T(4,128)(2,1)S(1)} %copy.58), channel_id=1, replica_groups=mesh['seq'=32,'dp'=8] {'seq'}, dimensions={1} | all-to-all | bytes 3145728 | tf_op jit(solution)/shard_map/all_to_all | solution.py:61
  127.8 0.8 copy.59
  128.6 1.1 copy-done.7
  129.7 0.7 fusion.13
  130.4 2.5 copy.61
  132.9 7.2 %all-to-all-start.3 = ((bf16[128,4,1536]{2,1,0:T(4,128)(2,1)}), bf16[128,4,1536]{2,1,0:T(4,128)(2,1)}, u32[]{:S(2)}, u32[]{:S(2)}) async-start(bf16[128,4,1536]{2,1,0:T(4,128)(2,1)} %copy.61), calls=%async_computation.3 | async-start | bytes 3145728 | tf_op jit(solution)/shard_map/all_to_all | solution.py:25
  140.1 0.8 slice_bitcast_fusion.1
  140.9 2.1 collective-permute-start
  143.0 6.2 %collective-permute-start.1 = (bf16[1,1536]{1,0:T(2,128)(2,1)S(1)}, bf16[1,1536]{1,0:T(2,128)(2,1)S(1)}, u32[]{:S(2)}, u32[]{:S(2)}) collective-permute-start(bf16[1,1536]{1,0:T(2,128)(2,1)S(1)} %get-tuple-element.42), channel_id=1, source_target_pairs={{8,0},{16,8},{24,16},{32,24},{40,32},{48,40},{56,48},{64,56},{72,6... | collective-permute-start | bytes 9224 | tf_op jit(solution)/shard_map/ppermute | solution.py:15
  149.3 20.2 %collective-permute-done = bf16[1,1536]{1,0:T(2,128)(2,1)S(1)} collective-permute-done((bf16[1,1536]{1,0:T(2,128)(2,1)S(1)}, bf16[1,1536]{1,0:T(2,128)(2,1)S(1)}, u32[]{:S(2)}, u32[]{:S(2)}) %collective-permute-start) | collective-permute-done | bytes 3104 | tf_op jit(solution)/shard_map/ppermute | solution.py:14
  169.5 1.9 maximum_convert_fusion
  171.4 5.5 all-to-all-done.3
  176.9 3.1 copy.62
  180.0 3.7 all_to_all.58
  183.7 2.6 fusion.9
  186.3 1.6 fusion.7
  187.9 1.1 copy-done.5
  189.1 0.7 fusion.11
  189.8 1.3 copy.53
  191.1 43.9 %all_to_all.64 = bf16[128,4,1536]{2,1,0:T(4,128)(2,1)S(1)} all-to-all(bf16[128,4,1536]{2,1,0:T(4,128)(2,1)S(1)} %copy.53), channel_id=1, replica_groups=mesh['seq'=32,'dp'=8] {'seq'}, dimensions={0} | all-to-all | bytes 3145728 | tf_op jit(solution)/shard_map/all_to_all | solution.py:25
  235.1 0.8 copy.54
  235.9 1.2 copy-done.9
  237.1 0.7 fusion.12
  237.8 1.3 copy.56
  239.2 42.8 %all_to_all.65 = bf16[128,4,1536]{2,1,0:T(4,128)(2,1)S(1)} all-to-all(bf16[128,4,1536]{2,1,0:T(4,128)(2,1)S(1)} %copy.56), channel_id=1, replica_groups=mesh['seq'=32,'dp'=8] {'seq'}, dimensions={0} | all-to-all | bytes 3145728 | tf_op jit(solution)/shard_map/all_to_all | solution.py:25
  282.7 2.3 reshape.55
  284.9 9.1 %convolution_bitcast_fusion = f32[1536,1536]{0,1:T(8,128)} fusion(f32[1,512,1536]{2,1,0:T(8,128)} %reshape.55, bf16[1,512,1536]{2,1,0:T(8,128)(2,1)} %param.7, bf16[1,512,1536]{2,1,0:T(8,128)(2,1)} %param.6), kind=kOutput, calls=%fused_computation | convolution fusion | flops 2418278400 | bytes 15728640 | tf_op jit(solution)/shard_map/dot_general | solution.py:105
  294.1 9.6 %copy.70 = f32[1536,1536]{1,0:T(8,128)} copy(f32[1536,1536]{0,1:T(8,128)} %convolution_bitcast_fusion) | data formatting | bytes 18874368
  303.9 0.8 fusion.27
  304.6 3.6 collective-permute-start.2
  308.2 4.7 collective-permute-start.3
  312.9 3.2 fusion.28
  316.1 75.9 %psum.28 = f32[3,1536]{1,0:T(4,128)} all-reduce(f32[3,1536]{1,0:T(4,128)S(1)} %pad_maximum_fusion), channel_id=1, replica_groups=mesh['seq'=32,'dp'=8] {'seq','dp'}, use_global_device_ids=true, to_apply=%region_3.0 | all-reduce | flops 4608 | bytes 36864 | tf_op jit(solution)/shard_map/psum | solution.py:114
  392.0 3.7 maximum_convert_fusion.1
  395.7 1.3 fusion.20
  397.0 2.2 reshape.52
  399.3 50.2 %reduce-scatter.4.cloned.1.call-done = f32[48,1536]{1,0:T(8,128)} async-done(((f32[1536,1536]{1,0:T(8,128)}), f32[48,1536]{1,0:T(8,128)}) %reduce-scatter.4.cloned.1.call-update) | async-done | bytes 294928
  449.5 2.2 copy.71
  451.7 9.8 %fusion.14 = bf16[1,512,1536]{2,1,0:T(8,128)(2,1)} fusion(bf16[1536,1536]{1,0:T(8,128)(2,1)} %all-gather.2.cloned.1.call-done, f32[514,1536]{1,0:T(8,128)} %maximum_convert_fusion.1, bf16[512,1536]{1,0:T(8,128)(2,1)S(1)} %bitcast.78, f32[512,1536]{1,0:T(8,128)} %reshape.52, bf16[1,512,1536]{2,1,0:T(8,128)(2,1)} %param.7, f32[1536]{0:T(1024)S(1)} %get-tuple-element.33, ...), kind=kOutput, calls=%fused_computation.31 | convolution fusion | flops 2424569856 | bytes 18892800 | tf_op jit(solution)/shard_map/dot_general | solution.py:100
  461.5 1.6 fusion.15
  463.0 125.0 %all-reduce.3.cloned.1.call-done = (f32[48,1536]{0,1:T(8,128)}, f32[4,128,128]{2,1,0:T(8,128)}, f32[4,128,128]{2,1,0:T(8,128)}) async-done(((f32[48,1536]{0,1:T(8,128)}, f32[4,128,128]{2,1,0:T(8,128)}, f32[4,128,128]{2,1,0:T(8,128)}), (f32[48,1536]{0,1:T(8,128)}, f32[4,128,128]{2,1,0:T(8,128)}, f32[4,128,128]{2,1,0:T(8,128)})) %all-reduce.3.cloned.1.call-update) | async-done | bytes 819216 | tf_op jit(solution)/shard_map/psum | solution.py:113
  588.0 2.1 copy.67
  590.2 1.7 copy.83
  591.8 0.7 copy.84
  (42 shorter events, 1.0 us)
Async XLA Ops:
  7.2 176.5 %copy-start = (bf16[4,128,128]{2,1,0:T(8,128)(2,1)S(1)}, bf16[4,128,128]{2,1,0:T(8,128)(2,1)}, u32[]{:S(2)}) copy-start(bf16[4,128,128]{2,1,0:T(8,128)(2,1)} %param.10) | copy-start | bytes 393220
  7.2 69.4 %all-gather.2.cloned.1.call-start = ((), (), s32[]{:S(2)}) async-start(), calls=%async_computation.5 | async-start | bytes 4866048 | tf_op jit(solution)/shard_map/all_gather | solution.py:54
  127.8 1.9 copy-start.12
  128.5 1.1 copy-start.7
  132.9 16.3 %copy-start.14 = (f32[3,1536]{1,0:T(4,128)S(1)}, f32[3,1536]{1,0:T(4,128)}, u32[]{:S(2)}) copy-start(f32[3,1536]{1,0:T(4,128)} %param.8) | copy-start | bytes 55300
  132.9 44.0 %all-to-all-start.3 = ((bf16[128,4,1536]{2,1,0:T(4,128)(2,1)}), bf16[128,4,1536]{2,1,0:T(4,128)(2,1)}, u32[]{:S(2)}, u32[]{:S(2)}) async-start(bf16[128,4,1536]{2,1,0:T(4,128)(2,1)} %copy.61), calls=%async_computation.3 | async-start | bytes 3145728 | tf_op jit(solution)/shard_map/all_to_all | solution.py:25
  140.1 309.4 %reduce-scatter.4.cloned.1.call-start = ((), (), s32[]{:S(2)}) async-start(), calls=%async_computation.6 | async-start | bytes 9732096
  140.9 28.6 %collective-permute-start = (bf16[1,1536]{1,0:T(2,128)(2,1)S(1)}, bf16[1,1536]{1,0:T(2,128)(2,1)S(1)}, u32[]{:S(2)}, u32[]{:S(2)}) collective-permute-start(bf16[1,1536]{1,0:T(2,128)(2,1)S(1)} %get-tuple-element.41), channel_id=1, source_target_pairs={{0,8},{8,16},{16,24},{24,32},{32,40},{40,48},{48,56},{56,64},{64,7... | collective-permute-start | bytes 9224 | tf_op jit(solution)/shard_map/ppermute | solution.py:14
  143.0 26.5 %collective-permute-start.1 = (bf16[1,1536]{1,0:T(2,128)(2,1)S(1)}, bf16[1,1536]{1,0:T(2,128)(2,1)S(1)}, u32[]{:S(2)}, u32[]{:S(2)}) collective-permute-start(bf16[1,1536]{1,0:T(2,128)(2,1)S(1)} %get-tuple-element.42), channel_id=1, source_target_pairs={{8,0},{16,8},{24,16},{32,24},{40,32},{48,40},{56,48},{64,56},{72,6... | collective-permute-start | bytes 9224 | tf_op jit(solution)/shard_map/ppermute | solution.py:15
  183.7 2.6 copy-start.2
  186.3 1.6 copy-start.3
  187.9 1.2 copy-start.5
  235.8 1.2 copy-start.9
  303.8 284.3 %all-reduce.3.cloned.1.call-start = ((), (), s32[]{:S(2)}) async-start(), calls=%async_computation.7 | async-start | bytes 2621440 | tf_op jit(solution)/shard_map/psum | solution.py:113
  304.6 87.4 %collective-permute-start.2 = (bf16[1,1536]{1,0:T(2,128)(2,1)S(1)}, bf16[1,1536]{1,0:T(2,128)(2,1)S(1)}, u32[]{:S(2)}, u32[]{:S(2)}) collective-permute-start(bf16[1,1536]{1,0:T(2,128)(2,1)S(1)} %get-tuple-element.39), channel_id=1, source_target_pairs={{0,8},{8,16},{16,24},{24,32},{32,40},{40,48},{48,56},{56,64},{64,7... | collective-permute-start | bytes 9224 | tf_op jit(solution)/shard_map/ppermute | solution.py:14
  308.2 83.8 %collective-permute-start.3 = (bf16[1,1536]{1,0:T(2,128)(2,1)S(1)}, bf16[1,1536]{1,0:T(2,128)(2,1)S(1)}, u32[]{:S(2)}, u32[]{:S(2)}) collective-permute-start(bf16[1,1536]{1,0:T(2,128)(2,1)S(1)} %get-tuple-element.40), channel_id=1, source_target_pairs={{8,0},{16,8},{24,16},{32,24},{40,32},{48,40},{56,48},{64,56},{72,6... | collective-permute-start | bytes 9224 | tf_op jit(solution)/shard_map/ppermute | solution.py:15
  392.0 3.8 copy-start.8
  392.0 3.8 copy-start.10
  399.3 52.4 %copy-start.4 = (bf16[4,1536,128]{1,2,0:T(8,128)(2,1)S(1)}, bf16[4,1536,128]{1,2,0:T(8,128)(2,1)}, u32[]{:S(2)}) copy-start(bf16[4,1536,128]{1,2,0:T(8,128)(2,1)} %copy-done.3) | copy-start | bytes 4718596
  451.6 9.8 %copy-start.6 = (f32[512,1536]{1,0:T(8,128)S(1)}, f32[512,1536]{1,0:T(8,128)}, u32[]{:S(2)}) copy-start(f32[512,1536]{1,0:T(8,128)} %reshape.52) | copy-start | bytes 9437188
  451.7 9.8 %copy-start.11 = (f32[512,1536]{1,0:T(8,128)S(1)}, f32[512,1536]{1,0:T(8,128)}, u32[]{:S(2)}) copy-start(f32[512,1536]{1,0:T(8,128)} %get-tuple-element.44) | copy-start | bytes 9437188
  461.5 131.1 %copy-start.1 = (bf16[4,128,128]{2,1,0:T(8,128)(2,1)S(1)}, bf16[4,128,128]{2,1,0:T(8,128)(2,1)}, u32[]{:S(2)}) copy-start(bf16[4,128,128]{2,1,0:T(8,128)(2,1)} %param.10) | copy-start | bytes 393220
  588.0 3.8 copy-start.13
Sparse Core Ops, SparseCore 0:
  9.9 66.6 all-gather.1
  303.9 145.5 reduce-scatter.3
  452.9 135.0 all-reduce.2
where the time goes:
time: 600 us; the launch traced here: 599 us
  waiting for transfers between devices  270 us (45%)
  blocking collectives  205 us (34%)
  local copies, waits for them, and re-layouts  41 us (7%)
  matrix products  35.8 us (6%)
  starting transfers between devices  23.9 us (4%)
  between operations  14 us (2%)
  other arithmetic  9.23 us (2%)
    psum x1, waiting for transfers between devices, shards(): grad_gate = lax.psum(weight_part, 'dp')  125 us
    all_to_all x2, blocking collectives, regroup(): lax.all_to_all(values, 'seq', split_axis=0, concat_axis=1, tiled=True)  86.7 us
    psum x1, blocking collectives, shards(): grad_conv = lax.psum(conv_part, ('seq', 'dp'))  75.9 us
    all_gather x1, waiting for transfers between devices, shards(): whole_gate = lax.all_gather(gate_weight, 'seq', axis=0, tiled=True)  68.7 us
    unnamed x4, waiting for transfers between devices  50.9 us
    all_to_all x1, blocking collectives, shards(): lax.all_to_all(d_monarch.reshape(local_blocks, block_size, feat_width), '...  42.4 us
    ppermute x2, waiting for transfers between devices, with_halo(): before = lax.ppermute(last, axis, up)  20.2 us
    unnamed x35, local copies, waits for them, and re-layouts  19.9 us
  transfers between devices with their start and end apart: 8, of which 5 were waited for; matrix products, arithmetic and copies ran while one was open for 4% of the time, Pallas kernels for 0%

commit v1 on v0

--- a/solution.py
+++ b/solution.py
@@ -2,6 +2,10 @@
 import jax.numpy as jnp
 from jax import lax
 from jax.sharding import PartitionSpec as P
+
+
+def try_all_strings_up(row_data):
+    return jnp.sum(lax.all_gather(row_data, axis_name=("seq", "dp")), 0)
 
 
 def with_halo(array, sides, width):
@@ -111,7 +115,7 @@
     )
     grad_first, trailing_factor_gradient = lax.psum((grad_first, trailing_factor_gradient), "dp")
     grad_gate = lax.psum(weight_part, "dp")
-    grad_conv = lax.psum(conv_part, ("seq", "dp"))
+    grad_conv = try_all_strings_up(conv_part)
     return (
         mixed[None],
         grad_tokens[None],

time: 600 us -> 1320 us (2.20)
  waiting for transfers between devices: 270 us -> 1060 us
  blocking collectives: 205 us -> 129 us
    all_gather x0 -> x1, waiting for transfers between devices: none -> 717 us  [try_all_strings_up(): return jnp.sum(lax.all_gather(row_data, axis_name=('seq', 'dp')), 0)]
    psum x1 -> x0, blocking collectives: 75.9 us -> none  [shards(): grad_conv = lax.psum(conv_part, ('seq', 'dp'))]
    unnamed x4 -> x5, waiting for transfers between devices: 50.9 us -> 127 us
  transfers between devices with their start and end apart: 8 -> 9, of which waited for: 5 -> 6; matrix products, arithmetic and copies ran while one was open for 4% -> 2% of each run, Pallas kernels for 0% -> 0%
where the time goes in v1:
time: 1320 us
  waiting for transfers between devices  1060 us (80%)
  blocking collectives  129 us (10%)
  local copies, waits for them, and re-layouts  41.7 us (3%)
  matrix products  36 us (3%)
  starting transfers between devices  24.2 us (2%)
  between operations  14.1 us (1%)
    all_gather x1, waiting for transfers between devices, try_all_strings_up(): return jnp.sum(lax.all_gather(row_data, axis_name=('seq', 'dp')), 0)  717 us
    unnamed x5, waiting for transfers between devices  127 us
    psum x1, waiting for transfers between devices, shards(): grad_gate = lax.psum(weight_part, 'dp')  120 us
    all_to_all x2, blocking collectives, regroup(): lax.all_to_all(values, 'seq', split_axis=0, concat_axis=1, tiled=True)  86.7 us
    all_gather x1, waiting for transfers between devices, shards(): whole_gate = lax.all_gather(gate_weight, 'seq', axis=0, tiled=True)  68.7 us
    all_to_all x1, blocking collectives, shards(): lax.all_to_all(d_monarch.reshape(local_blocks, block_size, feat_width), '...  42.4 us
  transfers between devices with their start and end apart: 9, of which 6 were waited for; matrix products, arithmetic and copies ran while one was open for 2% of the time, Pallas kernels for 0%

profile of v1, /device:TPU:2, one launch (start us, length us, event | category | flops | bytes accessed | tf_op | source)
XLA Modules:
  0.0 1315.4 jit_solution(11920066574276222416)
XLA Ops:
  7.9 68.7 %all-gather.5.cloned.1.call-done = bf16[1536,1536]{1,0:T(8,128)(2,1)} async-done(((bf16[48,1536]{1,0:T(8,128)(2,1)}), bf16[1536,1536]{1,0:T(8,128)(2,1)}) %all-gather.5.cloned.1.call-update) | async-done | bytes 4718608 | tf_op jit(solution)/shard_map/all_gather | solution.py:58
  76.6 7.6 fusion.2
  84.2 1.2 copy.58
  85.4 42.4 %all_to_all.63 = bf16[4,128,1536]{2,0,1:T(4,128)(2,1)S(1)} all-to-all(bf16[4,128,1536]{2,0,1:T(4,128)(2,1)S(1)} %copy.58), channel_id=1, replica_groups=mesh['seq'=32,'dp'=8] {'seq'}, dimensions={1} | all-to-all | bytes 3145728 | tf_op jit(solution)/shard_map/all_to_all | solution.py:65
  127.8 0.8 copy.59
  128.6 1.1 copy-done.8
  129.7 0.7 fusion.13
  130.5 2.5 copy.61
  132.9 7.2 all-to-all-start.3
  140.2 0.8 slice_bitcast_fusion.1
  141.0 2.1 collective-permute-start
  143.0 6.2 collective-permute-start.1
  149.3 20.2 %collective-permute-done = bf16[1,1536]{1,0:T(2,128)(2,1)S(1)} collective-permute-done((bf16[1,1536]{1,0:T(2,128)(2,1)S(1)}, bf16[1,1536]{1,0:T(2,128)(2,1)S(1)}, u32[]{:S(2)}, u32[]{:S(2)}) %collective-permute-start) | collective-permute-done | bytes 3104 | tf_op jit(solution)/shard_map/ppermute | solution.py:18
  169.6 1.9 maximum_convert_fusion
  171.5 5.5 all-to-all-done.3
  176.9 3.1 copy.62
  180.0 3.7 all_to_all.58
  183.7 2.6 fusion.9
  186.4 1.6 fusion.7
  188.0 1.1 copy-done.6
  189.1 0.7 fusion.11
  189.8 1.3 copy.53
  191.2 43.9 %all_to_all.64 = bf16[128,4,1536]{2,1,0:T(4,128)(2,1)S(1)} all-to-all(bf16[128,4,1536]{2,1,0:T(4,128)(2,1)S(1)} %copy.53), channel_id=1, replica_groups=mesh['seq'=32,'dp'=8] {'seq'}, dimensions={0} | all-to-all | bytes 3145728 | tf_op jit(solution)/shard_map/all_to_all | solution.py:29
  235.1 0.8 copy.54
  235.9 1.1 copy-done.10
  237.1 0.7 fusion.12
  237.8 1.3 copy.56
  239.1 42.8 %all_to_all.65 = bf16[128,4,1536]{2,1,0:T(4,128)(2,1)S(1)} all-to-all(bf16[128,4,1536]{2,1,0:T(4,128)(2,1)S(1)} %copy.56), channel_id=1, replica_groups=mesh['seq'=32,'dp'=8] {'seq'}, dimensions={0} | all-to-all | bytes 3145728 | tf_op jit(solution)/shard_map/all_to_all | solution.py:29
  282.7 2.3 reshape.55
  285.0 9.1 convolution_bitcast_fusion
  294.1 9.6 copy.70
  304.6 0.8 fusion.27
  305.4 3.6 collective-permute-start.2
  309.0 5.0 collective-permute-start.3
  314.0 3.3 fusion.28
  317.4 2.2 maximum_convert_fusion.1
  319.6 0.7 copy-done.11
  320.3 1.3 fusion.20
  321.6 2.3 reshape.52
  323.9 126.0 %reduce-scatter.4.cloned.1.call-done = f32[48,1536]{1,0:T(8,128)} async-done(((f32[1536,1536]{1,0:T(8,128)}), f32[48,1536]{1,0:T(8,128)}) %reduce-scatter.4.cloned.1.call-update) | async-done | bytes 294928
  449.9 2.1 copy.71
  452.1 9.8 fusion.14
  461.9 1.6 fusion.15
  463.4 716.7 %all-gather.7.cloned.1.call-done = f32[256,3,1536]{2,1,0:T(4,128)} async-done(((f32[1,3,1536]{2,1,0:T(4,128)}), f32[256,3,1536]{2,1,0:T(4,128)}) %all-gather.7.cloned.1.call-update) | async-done | bytes 4718608 | tf_op jit(solution)/shard_map/all_gather | solution.py:8
  1180.1 4.3 reduce_sum.39
  1184.5 119.8 %all-reduce.3.cloned.1.call-done = (f32[48,1536]{0,1:T(8,128)}, f32[4,128,128]{2,1,0:T(8,128)}, f32[4,128,128]{2,1,0:T(8,128)}) async-done(((f32[48,1536]{0,1:T(8,128)}, f32[4,128,128]{2,1,0:T(8,128)}, f32[4,128,128]{2,1,0:T(8,128)}), (f32[48,1536]{0,1:T(8,128)}, f32[4,128,128]{2,1,0:T(8,128)}, f32[4,128,128]{2,1,0:T(8,128)})) %all-reduce.3.cloned.1.call-update) | async-done | bytes 819216 | tf_op jit(solution)/shard_map/psum | solution.py:117
  1304.3 2.1 copy.67
  1306.4 1.7 copy.83
  (47 shorter events, 3.1 us)
Async XLA Ops:
  7.2 176.6 %copy-start = (bf16[4,128,128]{2,1,0:T(8,128)(2,1)S(1)}, bf16[4,128,128]{2,1,0:T(8,128)(2,1)}, u32[]{:S(2)}) copy-start(bf16[4,128,128]{2,1,0:T(8,128)(2,1)} %param.10) | copy-start | bytes 393220
  7.2 69.4 %all-gather.5.cloned.1.call-start = ((), (), s32[]{:S(2)}) async-start(), calls=%async_computation.5 | async-start | bytes 4866048 | tf_op jit(solution)/shard_map/all_gather | solution.py:58
  127.8 1.9 copy-start.13
  128.6 1.1 copy-start.8
  132.9 16.3 %copy-start.15 = (f32[3,1536]{1,0:T(4,128)S(1)}, f32[3,1536]{1,0:T(4,128)}, u32[]{:S(2)}) copy-start(f32[3,1536]{1,0:T(4,128)} %param.8) | copy-start | bytes 55300
  132.9 44.0 %all-to-all-start.3 = ((bf16[128,4,1536]{2,1,0:T(4,128)(2,1)}), bf16[128,4,1536]{2,1,0:T(4,128)(2,1)}, u32[]{:S(2)}, u32[]{:S(2)}) async-start(bf16[128,4,1536]{2,1,0:T(4,128)(2,1)} %copy.61), calls=%async_computation.3 | async-start | bytes 3145728 | tf_op jit(solution)/shard_map/all_to_all | solution.py:29
  140.1 309.7 %reduce-scatter.4.cloned.1.call-start = ((), (), s32[]{:S(2)}) async-start(), calls=%async_computation.7 | async-start | bytes 9732096
  141.0 28.6 %collective-permute-start = (bf16[1,1536]{1,0:T(2,128)(2,1)S(1)}, bf16[1,1536]{1,0:T(2,128)(2,1)S(1)}, u32[]{:S(2)}, u32[]{:S(2)}) collective-permute-start(bf16[1,1536]{1,0:T(2,128)(2,1)S(1)} %get-tuple-element.41), channel_id=1, source_target_pairs={{0,8},{8,16},{16,24},{24,32},{32,40},{40,48},{48,56},{56,64},{64,7... | collective-permute-start | bytes 9224 | tf_op jit(solution)/shard_map/ppermute | solution.py:18
  143.0 26.5 %collective-permute-start.1 = (bf16[1,1536]{1,0:T(2,128)(2,1)S(1)}, bf16[1,1536]{1,0:T(2,128)(2,1)S(1)}, u32[]{:S(2)}, u32[]{:S(2)}) collective-permute-start(bf16[1,1536]{1,0:T(2,128)(2,1)S(1)} %get-tuple-element.42), channel_id=1, source_target_pairs={{8,0},{16,8},{24,16},{32,24},{40,32},{48,40},{56,48},{64,56},{72,6... | collective-permute-start | bytes 9224 | tf_op jit(solution)/shard_map/ppermute | solution.py:19
  183.7 2.6 copy-start.2
  186.3 1.6 copy-start.3
  187.9 1.2 copy-start.6
  235.9 1.2 copy-start.10
  303.8 876.3 %all-gather.7.cloned.1.call-start = ((), (), s32[]{:S(2)}) async-start(), calls=%async_computation.6 | async-start | bytes 6316032 | tf_op jit(solution)/shard_map/all_gather | solution.py:8
  304.5 999.8 %all-reduce.3.cloned.1.call-start = ((), (), s32[]{:S(2)}) async-start(), calls=%async_computation.8 | async-start | bytes 2621440 | tf_op jit(solution)/shard_map/psum | solution.py:117
  305.4 12.0 collective-permute-start.2
  309.0 8.4 copy-start.4
  309.0 8.4 collective-permute-start.3
  317.4 2.2 copy-start.9
  317.4 2.9 copy-start.11
  323.9 128.2 %copy-start.5 = (bf16[4,1536,128]{1,2,0:T(8,128)(2,1)S(1)}, bf16[4,1536,128]{1,2,0:T(8,128)(2,1)}, u32[]{:S(2)}) copy-start(bf16[4,1536,128]{1,2,0:T(8,128)(2,1)} %copy-done.3) | copy-start | bytes 4718596
  452.1 9.8 copy-start.7
  452.1 9.8 copy-start.12
  1180.1 128.7 %copy-start.1 = (bf16[4,128,128]{2,1,0:T(8,128)(2,1)S(1)}, bf16[4,128,128]{2,1,0:T(8,128)(2,1)}, u32[]{:S(2)}) copy-start(bf16[4,128,128]{2,1,0:T(8,128)(2,1)} %param.10) | copy-start | bytes 393220
  1304.3 3.8 copy-start.14
Sparse Core Ops, SparseCore 0:
  9.9 66.6 all-gather.4
  303.9 145.9 reduce-scatter.3
  452.3 727.7 all-gather.6
  1183.4 120.8 all-reduce.2
